TPU v7x, 512 devices: a whole 4x4x16 slice. The times are simulated.
512 devices in a mesh: vec: 32 (over y_lo, z), gz: 16 (over x, y_hi, core).
Axes of the slice: x: 4, y: 4 (y_hi: 2, y_lo: 2; y = y_hi * 2 + y_lo), z: 16, core: 2. Of those that a mesh axis runs over, the one named last changes fastest.
Arguments:
- base_flow: float32 [3, 128, 128, 128], P(None, 'gz'), may hold values from -6 to 6
- tangents: float32 [32, 3, 128, 128, 128], P('vec', None, 'gz'), may hold values from -6 to 6
- shells: int32 [4], replicated, may hold values from 1 to 31
Outputs:
- base_next: float32 [3, 128, 128, 128], P(None, 'gz', 'vec')
- ortho_tangents: float32 [32, 3, 128, 128, 128], P('vec', None, 'gz')
- growth: float32 [32], replicated
Inputs may be any that keep to these rules, and one draw needn't show every extreme that they name: `shells`: repeats may occur.
All inputs are finite; a program needn't handle non-finite values.
Results may differ from a plain program's by a relative error of at most 0.00017.
Values sent between devices are 32-bit elements; how exact they have to be, the bound alone decides.
A program may use at most 128 MiB of HBM per device.

v0:
```python
import math

import jax
import jax.numpy as jnp
from jax import lax
from jax.sharding import PartitionSpec as P

NX = 128
NY = 128
NZ = 128


time_step = 0.005
viscosity = 0.01
forcing_amplitude = 4.0
highest = lax.Precision.HIGHEST


def padded_2(block, sides, width):
    for axis, dim in sides:
        count = lax.axis_size(axis)
        forward = [(i, i + 1) for i in range(count - 1)]
        forward.append((count - 1, 0))
        backward = [(target, source) for source, target in forward]
        low = lax.ppermute(
            lax.slice_in_dim(block, block.shape[dim] - width, None, axis=dim), axis, forward
        )
        high = lax.ppermute(lax.slice_in_dim(block, 0, width, axis=dim), axis, backward)
        block = jnp.concatenate([low, block, high], axis=dim)
    return block


def grid_spacing():
    return 2.0 * math.pi / NX


def dft_tables(length):
    indices = jnp.arange(length, dtype=jnp.int32)
    angles = (
        2.0 * math.pi / length * (indices[:, None] * indices[None, :] % length).astype(jnp.float32)
    )
    return (jnp.cos(angles), jnp.sin(angles))


def forward(real_in, imag_in):
    number, layers = (real_in.shape[0], real_in.shape[1])
    cos_x, sin_x = dft_tables(NX)
    cos_y, sin_y = dft_tables(NY)
    cos_z, sin_z = dft_tables(NZ)
    real_x = jnp.einsum("mzyx,xk->mzyk", real_in, cos_x, precision=highest) + jnp.einsum(
        "mzyx,xk->mzyk", imag_in, sin_x, precision=highest
    )
    imag_x = jnp.einsum("mzyx,xk->mzyk", imag_in, cos_x, precision=highest) - jnp.einsum(
        "mzyx,xk->mzyk", real_in, sin_x, precision=highest
    )
    real_y = jnp.einsum("mzyx,yk->mzkx", real_x, cos_y, precision=highest) + jnp.einsum(
        "mzyx,yk->mzkx", imag_x, sin_y, precision=highest
    )
    imag_y = jnp.einsum("mzyx,yk->mzkx", imag_x, cos_y, precision=highest) - jnp.einsum(
        "mzyx,yk->mzkx", real_x, sin_y, precision=highest
    )
    flat_shape = (number, layers, NY * NX)
    real_c, imag_c = (
        lax.all_to_all(real_y.reshape(flat_shape), "gz", split_axis=2, concat_axis=1, tiled=True),
        lax.all_to_all(imag_y.reshape(flat_shape), "gz", split_axis=2, concat_axis=1, tiled=True),
    )
    real_z = jnp.einsum("mzp,zk->mkp", real_c, cos_z, precision=highest) + jnp.einsum(
        "mzp,zk->mkp", imag_c, sin_z, precision=highest
    )
    imag_z = jnp.einsum("mzp,zk->mkp", imag_c, cos_z, precision=highest) - jnp.einsum(
        "mzp,zk->mkp", real_c, sin_z, precision=highest
    )
    return (real_z, imag_z)


def backward(real_z, imag_z, layers):
    number = real_z.shape[0]
    cos_x, sin_x = dft_tables(NX)
    cos_y, sin_y = dft_tables(NY)
    cos_z, sin_z = dft_tables(NZ)
    real_c = jnp.einsum("mkp,kz->mzp", real_z, cos_z, precision=highest) - jnp.einsum(
        "mkp,kz->mzp", imag_z, sin_z, precision=highest
    )
    imag_c = jnp.einsum("mkp,kz->mzp", imag_z, cos_z, precision=highest) + jnp.einsum(
        "mkp,kz->mzp", real_z, sin_z, precision=highest
    )
    real_s, imag_s = (
        lax.all_to_all(real_c, "gz", split_axis=1, concat_axis=2, tiled=True),
        lax.all_to_all(imag_c, "gz", split_axis=1, concat_axis=2, tiled=True),
    )
    real_s = real_s.reshape(number, layers, NY, NX)
    imag_s = imag_s.reshape(number, layers, NY, NX)
    real_y = jnp.einsum("mzkx,ky->mzyx", real_s, cos_y, precision=highest) - jnp.einsum(
        "mzkx,ky->mzyx", imag_s, sin_y, precision=highest
    )
    imag_y = jnp.einsum("mzkx,ky->mzyx", imag_s, cos_y, precision=highest) + jnp.einsum(
        "mzkx,ky->mzyx", real_s, sin_y, precision=highest
    )
    real_out = jnp.einsum("mzyk,kx->mzyx", real_y, cos_x, precision=highest) - jnp.einsum(
        "mzyk,kx->mzyx", imag_y, sin_x, precision=highest
    )
    imag_out = jnp.einsum("mzyk,kx->mzyx", imag_y, cos_x, precision=highest) + jnp.einsum(
        "mzyk,kx->mzyx", real_y, sin_x, precision=highest
    )
    scale = 1.0 / (NX * NY * NZ)
    return (real_out * scale, imag_out * scale)


def inverse_symbol(width):
    spacing = grid_spacing()
    wave_z = jnp.arange(NZ, dtype=jnp.int32)[:, None]
    flat_index = lax.axis_index("gz") * width + jnp.arange(width, dtype=jnp.int32)[None, :]
    wave_y = flat_index // NX
    wave_x = flat_index % NX

    def slope(wave, length):
        return jnp.sin(2.0 * math.pi / length * wave.astype(jnp.float32)) / spacing

    shape = (NZ, width)
    squared = jnp.broadcast_to(slope(wave_x, NX), shape) ** 2
    squared = squared + jnp.broadcast_to(slope(wave_y, NY), shape) ** 2
    squared = squared + jnp.broadcast_to(slope(wave_z, NZ), shape) ** 2
    resting = (wave_x % (NX // 2) == 0) & (wave_y % (NY // 2) == 0) & (wave_z % (NZ // 2) == 0)
    return jnp.where(resting, 0.0, 1.0 / jnp.where(resting, 1.0, squared))


def project_potential(inner, padded_rate, layers):
    spacing = grid_spacing()
    spread = jnp.roll(inner[:, 0], -1, 3) - jnp.roll(inner[:, 0], 1, 3)
    spread = spread + jnp.roll(inner[:, 1], -1, 2) - jnp.roll(inner[:, 1], 1, 2)
    spread = (spread + padded_rate[:, 2:] - padded_rate[:, :-2]) / (2.0 * spacing)
    real_z, imag_z = forward(spread[0::2], spread[1::2])
    inverse = inverse_symbol(real_z.shape[2])
    real_p, imag_p = backward(-real_z * inverse, -imag_z * inverse, layers)
    potential = jnp.stack([real_p, imag_p], axis=1).reshape(spread.shape)
    padded_phi = padded_2(potential, (("gz", 1),), 1)
    slope_x = (jnp.roll(potential, -1, 3) - jnp.roll(potential, 1, 3)) / (2.0 * spacing)
    slope_y = (jnp.roll(potential, -1, 2) - jnp.roll(potential, 1, 2)) / (2.0 * spacing)
    slope_z = (padded_phi[:, 2:] - padded_phi[:, :-2]) / (2.0 * spacing)
    return inner - jnp.stack([slope_x, slope_y, slope_z], axis=1)


def tendencies(velocity, tangent, shells, depth):
    spacing = grid_spacing()
    number, layers = (tangent.shape[0], tangent.shape[2])
    stacked = jnp.concatenate([velocity[None], tangent], axis=0).reshape(
        (number + 1) * 3, layers, NY, NX
    )
    padded = padded_2(stacked, (("gz", 1),), depth)
    interior = padded[:, 1:-1]
    extent = interior.shape[1]
    full_shape = (number + 1, 3, extent, NY, NX)
    slopes = [
        ((jnp.roll(interior, -1, 3) - jnp.roll(interior, 1, 3)) / (2.0 * spacing)).reshape(
            full_shape
        ),
        ((jnp.roll(interior, -1, 2) - jnp.roll(interior, 1, 2)) / (2.0 * spacing)).reshape(
            full_shape
        ),
        ((padded[:, 2:] - padded[:, :-2]) / (2.0 * spacing)).reshape(full_shape),
    ]
    laplacian = (
        jnp.roll(interior, -1, 3)
        + jnp.roll(interior, 1, 3)
        + jnp.roll(interior, -1, 2)
        + jnp.roll(interior, 1, 2)
    )
    laplacian = (
        (laplacian + padded[:, 2:] + padded[:, :-2] - 6.0 * interior) / (spacing * spacing)
    ).reshape(full_shape)
    fields = interior.reshape(full_shape)
    base_part_field = fields[0]
    tangent_field = fields[1:]
    positions = (
        lax.axis_index("gz") * layers - (depth - 1) + jnp.arange(extent, dtype=jnp.int32)
    ) % NZ
    angles = 2.0 * math.pi / NZ * (shells[:, None] * positions[None, :] % NZ).astype(jnp.float32)
    profile = forcing_amplitude * jnp.sum(jnp.sin(angles), axis=0)
    zeros = jnp.zeros((extent, NY, NX), jnp.float32)
    forcing = jnp.stack([jnp.broadcast_to(profile[:, None, None], (extent, NY, NX)), zeros, zeros])
    base_advect = jnp.zeros_like(base_part_field)
    tangent_advect = jnp.zeros_like(tangent_field)
    for direction in range(3):
        base_advect = base_advect + base_part_field[direction][None] * slopes[direction][0]
        tangent_advect = (
            tangent_advect + base_part_field[direction][None, None] * slopes[direction][1:]
        )
        tangent_advect = (
            tangent_advect + tangent_field[:, direction][:, None] * slopes[direction][0][None]
        )
    base_part = -base_advect + viscosity * laplacian[0] + forcing
    tangent_part = -tangent_advect + viscosity * laplacian[1:]
    return jnp.concatenate([base_part[None], tangent_part], axis=0)


def advance(velocity, tangent, shells):
    layers = velocity.shape[1]
    rates = tendencies(velocity, tangent, shells, 1)
    padded_rate = padded_2(rates[:, 2], (("gz", 1),), 1)
    rates = project_potential(rates, padded_rate, layers)
    return (velocity + time_step * rates[0], tangent + time_step * rates[1:])


def per_device(base_flow, tangents, shells):
    base_next, tangent_c = advance(base_flow, tangents, shells)
    row_count = NY // lax.axis_size("vec")
    base_rows = lax.dynamic_slice_in_dim(base_next, lax.axis_index("vec") * row_count, row_count, 2)
    flattened = tangent_c.reshape(tangents.shape[0], -1)
    cell_columns = lax.all_to_all(flattened, "vec", split_axis=1, concat_axis=0, tiled=True)
    partial_gram = jnp.dot(cell_columns, cell_columns.T, precision=highest)
    gram_matrix = lax.psum(partial_gram, ("vec", "gz")) / (3.0 * NZ * NY * NX)
    factor = jnp.linalg.cholesky(gram_matrix)
    ortho_rows = lax.linalg.triangular_solve(factor, cell_columns, left_side=True, lower=True)
    returned = lax.all_to_all(ortho_rows, "vec", split_axis=0, concat_axis=1, tiled=True)
    return (base_rows, returned.reshape(tangents.shape), jnp.log(jnp.diagonal(factor)))


def solution(mesh):
    in_specs = (P(None, "gz", None, None), P("vec", None, "gz", None, None), P())
    out_specs = (P(None, "gz", "vec", None), P("vec", None, "gz", None, None), P())
    return jax.shard_map(
        per_device, mesh=mesh, in_specs=in_specs, out_specs=out_specs, check_vma=False
    )
```

profile of v0, /device:TPU:32, one launch (start us, length us, event | category | flops | bytes accessed | tf_op | source)
XLA Modules:
  0.0 683.7 jit_solution(534279830836166000)
XLA Ops:
  3.7 6.7 collective-permute-start
  33.5 7.5 %subtract_multiply_fusion.3 = (f32[6,8,128,128]{3,2,1,0:T(8,128)S(1)}, f32[6,8,128,128]{3,2,1,0:T(8,128)}) fusion(f32[6,8,128,127]{3,2,1,0:T(8,128)} %get-tuple-element.15, f32[6,8,128,1]{3,2,1,0:T(8,128)} %get-tuple-element.17, f32[6,8,128,1]{3,2,1,0:T(8,128)} %get-tuple-element.16, f32[6,8,128,127]{3,2,1,0:T(8,128)} %get-tuple-element.14, ...), kind=kLoop, calls=%fused_computation.20 | loop fusion | flops 12582912 | bytes 22806528 | tf_op jit(solution)/shard_map/div | solution.py:154
  45.9 7.3 %collective-permute-start.2 = (f32[2,1,128,128]{3,2,1,0:T(8,128)S(1)}, f32[2,1,128,128]{3,2,1,0:T(8,128)S(1)}, u32[]{:S(2)}, u32[]{:S(2)}) collective-permute-start(f32[2,1,128,128]{3,2,1,0:T(8,128)S(1)} %get-tuple-element.48), channel_id=1, source_target_pairs={{1,0},{2,1},{3,2},{4,3},{5,4},{6,5},{7,6},{8,7},{9,8},{10,9},{11,1... | collective-permute-start | bytes 393224 | tf_op jit(solution)/shard_map/ppermute | solution.py:28
  55.7 7.4 %collective-permute-done.3 = f32[2,1,128,128]{3,2,1,0:T(8,128)S(1)} collective-permute-done((f32[2,1,128,128]{3,2,1,0:T(8,128)S(1)}, f32[2,1,128,128]{3,2,1,0:T(8,128)S(1)}, u32[]{:S(2)}, u32[]{:S(2)}) %collective-permute-start.3) | collective-permute-done | bytes 131104 | tf_op jit(solution)/shard_map/ppermute | solution.py:25
  70.7 5.9 copy.158
  77.1 74.5 %reduce.8 = f32[16384,8]{1,0:T(8,128)} reduce(f32[16384,1,8]{2,1,0:T(1,128)} %bitcast.207, f32[]{:T(128)} %broadcast.594), dimensions={1}, to_apply=%bitcast.180.reduce_sub_computation | reduce | bytes 1048580
  151.5 7.3 %reshape.513 = f32[16,1,8192]{2,1,0:T(1,128)} reshape(f32[16384,8]{1,0:T(8,128)} %reduce.8) | data formatting | bytes 1048576
  158.8 4.4 all-to-all-start
  167.9 5.9 copy.162
  173.8 74.5 %reduce.6 = f32[16384,8]{1,0:T(8,128)} reduce(f32[16384,1,8]{2,1,0:T(1,128)} %bitcast.208, f32[]{:T(128)} %broadcast.594), dimensions={1}, to_apply=%bitcast.178.reduce_sub_computation | reduce | bytes 1048580
  248.3 7.3 %reshape.511 = f32[16,1,8192]{2,1,0:T(1,128)} reshape(f32[16384,8]{1,0:T(8,128)} %reduce.6) | data formatting | bytes 1048576
  255.6 7.7 %all-to-all-start.1 = ((f32[16,1,8192]{2,1,0:T(1,128)}), f32[16,1,8192]{2,1,0:T(1,128)}, u32[]{:S(2)}, u32[]{:S(2)}) async-start(f32[16,1,8192]{2,1,0:T(1,128)} %reshape.511), calls=%async_computation.1 | async-start | bytes 1048576 | tf_op jit(solution)/shard_map/all_to_all | solution.py:65
  267.2 18.4 %reshape.514 = f32[16384,1,8]{2,1,0:T(1,128)} reshape(f32[16,8192]{1,0:T(8,128)} %reduce.9) | data formatting | bytes 1048576
  285.6 5.8 copy.159
  298.2 18.6 %reshape.512 = f32[16384,1,8]{2,1,0:T(1,128)} reshape(f32[16,8192]{1,0:T(8,128)} %reduce.7) | data formatting | bytes 1048576
  316.8 5.9 copy.163
  332.3 7.6 %all-to-all-start.2 = ((f32[1,128,1024]{2,0,1:T(1,128)}), f32[1,128,1024]{2,0,1:T(1,128)}, u32[]{:S(2)}, u32[]{:S(2)}) async-start(f32[1,128,1024]{2,0,1:T(1,128)} %copy.129), calls=%async_computation.2 | async-start | bytes 1048576 | tf_op jit(solution)/shard_map/all_to_all | solution.py:88
  345.1 7.2 %all-to-all-done.2 = f32[1,128,1024]{2,0,1:T(1,128)} async-done(((f32[1,128,1024]{2,0,1:T(1,128)}), f32[1,128,1024]{2,0,1:T(1,128)}, u32[]{:S(2)}, u32[]{:S(2)}) %all-to-all-start.2) | async-done | bytes 524320 | tf_op jit(solution)/shard_map/all_to_all | solution.py:88
  363.3 5.5 all-to-all-done.3
  387.6 6.5 collective-permute-done.5
  396.2 89.2 %all_to_all.89 = f32[1,32,12288]{2,0,1:T(1,128)S(1)} all-to-all(f32[1,32,12288]{2,0,1:T(1,128)S(1)} %bitcast.213), channel_id=1, replica_groups=mesh['vec'=32,'gz'=16] {'vec'}, dimensions={1} | all-to-all | bytes 3145728 | tf_op jit(solution)/shard_map/all_to_all | solution.py:209
  487.6 99.1 %psum.7 = f32[32,32]{0,1:T(8,128)S(1)} all-reduce(f32[32,32]{0,1:T(8,128)S(1)} %fusion.15), channel_id=1, replica_groups=mesh['vec'=32,'gz'=16] {'vec','gz'}, use_global_device_ids=true, to_apply=%region_1.2 | all-reduce | flops 1024 | bytes 8192 | tf_op jit(solution)/shard_map/psum | solution.py:211
  598.5 6.5 all-to-all-start.5
  607.8 74.3 %all-to-all-done.5 = f32[32,1,12288]{2,1,0:T(1,128)S(1)} async-done(((f32[32,1,12288]{2,1,0:T(1,128)}), f32[32,1,12288]{2,1,0:T(1,128)S(1)}, u32[]{:S(2)}, u32[]{:S(2)}) %all-to-all-start.5) | async-done | bytes 1572896 | tf_op jit(solution)/shard_map/all_to_all | solution.py:214
  (128 shorter events, 121.0 us)
Async XLA Ops:
  3.7 26.9 %collective-permute-start = (f32[6,1,128,128]{3,2,1,0:T(8,128)}, f32[6,1,128,128]{3,2,1,0:T(8,128)S(1)}, u32[]{:S(2)}, u32[]{:S(2)}) collective-permute-start(f32[6,1,128,128]{3,2,1,0:T(8,128)} %get-tuple-element.19), channel_id=1, source_target_pairs={{1,0},{2,1},{3,2},{4,3},{5,4},{6,5},{7,6},{8,7},{9,8},{10,9},{11,1... | collective-permute-start | bytes 1179656 | tf_op jit(solution)/shard_map/ppermute | solution.py:28
  10.4 20.2 %collective-permute-start.1 = (f32[6,1,128,128]{3,2,1,0:T(8,128)}, f32[6,1,128,128]{3,2,1,0:T(8,128)}, u32[]{:S(2)}, u32[]{:S(2)}) collective-permute-start(f32[6,1,128,128]{3,2,1,0:T(8,128)} %get-tuple-element.18), channel_id=1, source_target_pairs={{0,1},{1,2},{2,3},{3,4},{4,5},{5,6},{6,7},{7,8},{8,9},{9,10},{10,1... | collective-permute-start | bytes 1179656 | tf_op jit(solution)/shard_map/ppermute | solution.py:25
  16.2 3.8 copy-start.4
  20.0 2.0 copy-start.2
  20.0 3.2 copy-start.15
  30.6 2.0 copy-start
  30.6 3.0 copy-start.1
  30.6 3.0 copy-start.13
  30.6 3.0 copy-start.14
  33.5 7.6 %copy-start.11 = (f32[8,128,128]{2,1,0:T(8,128)S(1)}, f32[8,128,128]{2,1,0:T(8,128)}, u32[]{:S(2)}) copy-start(f32[8,128,128]{2,1,0:T(8,128)} %get-tuple-element.24) | copy-start | bytes 1572868
  33.5 7.6 %copy-start.12 = (f32[8,128,128]{2,1,0:T(8,128)S(1)}, f32[8,128,128]{2,1,0:T(8,128)}, u32[]{:S(2)}) copy-start(f32[8,128,128]{2,1,0:T(8,128)} %get-tuple-element.25) | copy-start | bytes 1572868
  45.9 9.8 %collective-permute-start.2 = (f32[2,1,128,128]{3,2,1,0:T(8,128)S(1)}, f32[2,1,128,128]{3,2,1,0:T(8,128)S(1)}, u32[]{:S(2)}, u32[]{:S(2)}) collective-permute-start(f32[2,1,128,128]{3,2,1,0:T(8,128)S(1)} %get-tuple-element.48), channel_id=1, source_target_pairs={{1,0},{2,1},{3,2},{4,3},{5,4},{6,5},{7,6},{8,7},{9,8},{10,9},{11,1... | collective-permute-start | bytes 393224 | tf_op jit(solution)/shard_map/ppermute | solution.py:28
  53.2 9.9 %collective-permute-start.3 = (f32[2,1,128,128]{3,2,1,0:T(8,128)S(1)}, f32[2,1,128,128]{3,2,1,0:T(8,128)S(1)}, u32[]{:S(2)}, u32[]{:S(2)}) collective-permute-start(f32[2,1,128,128]{3,2,1,0:T(8,128)S(1)} %get-tuple-element.49), channel_id=1, source_target_pairs={{0,1},{1,2},{2,3},{3,4},{4,5},{5,6},{6,7},{7,8},{8,9},{9,10},{10,1... | collective-permute-start | bytes 393224 | tf_op jit(solution)/shard_map/ppermute | solution.py:25
  66.4 1.7 copy-start.5
  158.8 96.8 %all-to-all-start = ((f32[16,1,8192]{2,1,0:T(1,128)}), f32[16,1,8192]{2,1,0:T(1,128)}, u32[]{:S(2)}, u32[]{:S(2)}) async-start(f32[16,1,8192]{2,1,0:T(1,128)} %reshape.513), calls=%async_computation | async-start | bytes 1048576 | tf_op jit(solution)/shard_map/all_to_all | solution.py:64
  255.6 38.8 %all-to-all-start.1 = ((f32[16,1,8192]{2,1,0:T(1,128)}), f32[16,1,8192]{2,1,0:T(1,128)}, u32[]{:S(2)}, u32[]{:S(2)}) async-start(f32[16,1,8192]{2,1,0:T(1,128)} %reshape.511), calls=%async_computation.1 | async-start | bytes 1048576 | tf_op jit(solution)/shard_map/all_to_all | solution.py:65
  322.6 5.5 copy-start.8
  327.2 2.1 copy-start.9
  332.3 20.0 %all-to-all-start.2 = ((f32[1,128,1024]{2,0,1:T(1,128)}), f32[1,128,1024]{2,0,1:T(1,128)}, u32[]{:S(2)}, u32[]{:S(2)}) async-start(f32[1,128,1024]{2,0,1:T(1,128)} %copy.129), calls=%async_computation.2 | async-start | bytes 1048576 | tf_op jit(solution)/shard_map/all_to_all | solution.py:88
  352.3 16.6 %all-to-all-start.3 = ((f32[1,128,1024]{2,0,1:T(1,128)}), f32[1,128,1024]{2,0,1:T(1,128)}, u32[]{:S(2)}, u32[]{:S(2)}) async-start(f32[1,128,1024]{2,0,1:T(1,128)} %copy.132), calls=%async_computation.3 | async-start | bytes 1048576 | tf_op jit(solution)/shard_map/all_to_all | solution.py:89
  373.0 4.9 copy-start.7
  382.3 5.3 collective-permute-start.4
  384.2 9.9 %collective-permute-start.5 = (f32[2,1,128,128]{3,2,1,0:T(8,128)S(1)}, f32[2,1,128,128]{3,2,1,0:T(8,128)S(1)}, u32[]{:S(2)}, u32[]{:S(2)}) collective-permute-start(f32[2,1,128,128]{3,2,1,0:T(8,128)S(1)} %get-tuple-element.39), channel_id=1, source_target_pairs={{0,1},{1,2},{2,3},{3,4},{4,5},{5,6},{6,7},{7,8},{8,9},{9,10},{10,1... | collective-permute-start | bytes 393224 | tf_op jit(solution)/shard_map/ppermute | solution.py:25
  598.5 83.6 %all-to-all-start.5 = ((f32[32,1,12288]{2,1,0:T(1,128)}), f32[32,1,12288]{2,1,0:T(1,128)S(1)}, u32[]{:S(2)}, u32[]{:S(2)}) async-start(f32[32,1,12288]{2,1,0:T(1,128)} %copy.145), calls=%async_computation.5 | async-start | bytes 3145728 | tf_op jit(solution)/shard_map/all_to_all | solution.py:214
  (3 other events, 3.0 us)
where the time goes:
time: 692 us; the launch traced here: 684 us
  blocking collectives  188 us (27%)
  other arithmetic  186 us (27%)
  local copies, waits for them, and re-layouts  113 us (16%)
  waiting for transfers between devices  101 us (15%)
  starting transfers between devices  53.1 us (8%)
  matrix products  40.1 us (6%)
    unnamed x2, other arithmetic  149 us
    psum x1, blocking collectives, per_device(): gram_matrix = lax.psum(partial_gram, ('vec', 'gz')) / (3.0 * NZ * NY * NX)  99.1 us
    all_to_all x1, blocking collectives, per_device(): lax.all_to_all(flattened, 'vec', split_axis=1, concat_axis=0, tiled=True)  89.2 us
    all_to_all x1, waiting for transfers between devices, per_device(): lax.all_to_all(ortho_rows, 'vec', split_axis=0, concat_axis=1, tiled=True)  74.3 us
    unnamed x38, local copies, waits for them, and re-layouts  57.9 us
    ppermute x3, starting transfers between devices, padded_2(): lax.ppermute(lax.slice_in_dim(block, 0, width, axis=dim), axis, backward)  15.9 us
    ppermute x3, waiting for transfers between devices, padded_2(): lax.ppermute(lax.slice_in_dim(block, block.shape[dim] - width, None, axis...  13.9 us
  transfers between devices with their start and end apart: 11, of which 6 were waited for; matrix products, arithmetic and copies ran while one was open for 23% of the time, Pallas kernels for 0%

commit v1 on v0

v1 whole, which is shorter than its diff:
```python
import functools
import math

import jax
import jax.numpy as jnp
import numpy as np
from jax import lax
from jax.experimental import pallas as pl
from jax.experimental.pallas import tpu as pltpu
from jax.sharding import PartitionSpec as P

N = 128
GZ = 16
NV = 32
LZ = N // GZ
ROWS = 3 * LZ * N // NV
time_step = 0.005
viscosity = 0.01
forcing_amplitude = 4.0
spacing = 2.0 * math.pi / N
half_inv = 1.0 / (2.0 * spacing)
lap_scale = viscosity / (spacing * spacing)
f32, bf16 = jnp.float32, jnp.bfloat16
MESH = pl.DeviceIdType.MESH


def tables():
    k = np.arange(N)
    angle = 2.0 * np.pi / N * ((k[:, None] * k[None, :]) % N)
    c, s = np.cos(angle), np.sin(angle)
    a = np.block([[c, -s], [s, c]]).astype(np.float32)
    hi = a.astype(jnp.bfloat16)
    lo = (a - hi.astype(np.float32)).astype(jnp.bfloat16)
    sine = np.sin(2.0 * np.pi / N * k)
    sine[[0, 64]] = 0.0
    slope2 = ((sine / spacing) ** 2).astype(np.float32)
    return hi, lo, np.ascontiguousarray(hi.T), np.ascontiguousarray(lo.T), sine.astype(np.float32), slope2


def split(x):
    hi = x.astype(bf16)
    return hi, (x - hi.astype(f32)).astype(bf16)


def dot(a, b):
    return jnp.dot(a, b, preferred_element_type=f32)


def right(x, hi, lo):
    xh, xl = split(x)
    return dot(xh, hi) + (dot(xl, hi) + dot(xh, lo))


def left(hi, lo, x):
    xh, xl = split(x)
    return dot(hi, xh) + (dot(hi, xl) + dot(lo, xh))


def up(x, axis):
    return pltpu.roll(x, N - 1, axis)


def down(x, axis):
    return pltpu.roll(x, 1, axis)


def kernel(shells, sine, base, tang, ahi, alo, bhi, blo, s2row, s2col,
           base_out, ortho, growth,
           E, Rt, S, T, T2, S2, Pf, V, BN, R, X, O2, gbuf, gsend, grecv, vsend, vrecv,
           lsem, hs, hr, a1s, a1r, a2s, a2r, ps, pr, vs, vr, gs, gr, ws, wr, os_, or_):
    v = lax.axis_index("vec")
    g = lax.axis_index("gz")
    nxt = lax.rem(g + 1, GZ)
    prv = lax.rem(g + GZ - 1, GZ)

    def zpeer(i):
        return lax.rem(g + i, GZ)

    def vpeer(i):
        return lax.rem(v + i, NV)

    barrier = pltpu.get_barrier_semaphore()

    @pl.loop(1, GZ)
    def _(i):
        pl.semaphore_signal(barrier, inc=1, device_id=(v, zpeer(i)), device_id_type=MESH)

    @pl.loop(1, NV)
    def _(i):
        pl.semaphore_signal(barrier, inc=1, device_id=(vpeer(i), g), device_id_type=MESH)

    load0 = pltpu.make_async_copy(base, E.at[0:3, 2:10], lsem.at[0])
    load1 = pltpu.make_async_copy(tang, E.at[3:6, 2:10], lsem.at[1])
    load0.start()
    load1.start()
    pl.semaphore_wait(barrier, GZ + NV - 2)

    halos = []
    for f, src in ((0, base), (3, tang)):
        for who, a, b in ((nxt, (LZ - 1, LZ - 2), (1, 0)), (prv, (0, 0), (10, 10))):
            n = len(halos)
            halos.append(pltpu.make_async_remote_copy(
                src.at[0:2, a[0]:a[0] + 1], E.at[f:f + 2, b[0]:b[0] + 1],
                hs.at[n], hr.at[n], device_id=(v, who), device_id_type=MESH))
            n += 1
            halos.append(pltpu.make_async_remote_copy(
                src.at[2, a[1]:a[1] + 2], E.at[f + 2, b[1]:b[1] + 2],
                hs.at[n], hr.at[n], device_id=(v, who), device_id_type=MESH))
    for h in halos:
        h.start()
    load0.wait()
    load1.wait()

    def rates(e, comps):
        bx, by, bz = E[0, e], E[1, e], E[2, e]
        tx, ty, tz = E[3, e], E[4, e], E[5, e]
        for c in comps:
            f = E[c, e]
            xp, xm, yp, ym, zp, zm = up(f, 1), down(f, 1), up(f, 0), down(f, 0), E[c, e + 1], E[c, e - 1]
            dx, dy, dz = xp - xm, yp - ym, zp - zm
            if comps != (2,):
                pass
            lap = ((xp + xm) + (yp + ym)) + (zp + zm) - 6.0 * f
            brate = lap * lap_scale - (bx * dx + by * dy + bz * dz) * half_inv
            if c == 0:
                zz = g * LZ + (e - 2)
                prof = 0.0
                for j in range(4):
                    prof = prof + sine[lax.rem(shells[j] * zz, N)]
                brate = brate + prof * forcing_amplitude
            Rt[c, e - 1] = brate
            adv = tx * dx + ty * dy + tz * dz
            f = E[c + 3, e]
            xp, xm, yp, ym, zp, zm = up(f, 1), down(f, 1), up(f, 0), down(f, 0), E[c + 3, e + 1], E[c + 3, e - 1]
            lap = ((xp + xm) + (yp + ym)) + (zp + zm) - 6.0 * f
            adv = adv + (bx * (xp - xm) + by * (yp - ym) + bz * (zp - zm))
            Rt[c + 3, e - 1] = lap * lap_scale - adv * half_inv

    @pl.loop(3, 9)
    def _(e):
        rates(e, (0, 1, 2))

    for h in halos:
        h.wait()

    @pl.loop(0, 2)
    def _(i):
        rates(2 + 7 * i, (0, 1, 2))

    @pl.loop(0, 2)
    def _(i):
        rates(1 + 9 * i, (2,))

    @pl.loop(0, LZ // 2)
    def _(p):
        parts = []
        for q in range(2):
            r = 2 * p + q + 1
            div = []
            for f in (0, 3):
                rx, ry = Rt[f, r], Rt[f + 1, r]
                d = (up(rx, 1) - down(rx, 1)) + (up(ry, 0) - down(ry, 0)) + (Rt[f + 2, r + 1] - Rt[f + 2, r - 1])
                div.append(d * half_inv)
            parts.append(right(jnp.concatenate(div, axis=1), ahi[...], alo[...]))
        rhs = jnp.concatenate([
            jnp.concatenate([parts[0][:, :N], parts[1][:, :N]], axis=1),
            jnp.concatenate([parts[0][:, N:], parts[1][:, N:]], axis=1)], axis=0)
        y = left(bhi[...], blo[...], rhs)
        for q in range(2):
            z8 = pl.multiple_of((2 * p + q) * 8, 8)
            for r in range(2):
                S[:, r, pl.ds(z8, 8), :] = y[r * N:(r + 1) * N, q * N:(q + 1) * N].reshape(GZ, 8, N)

    def a2a1(i):
        p = zpeer(i)
        return pltpu.make_async_remote_copy(
            S.at[p], T.at[:, pl.ds(pl.multiple_of(g * 64, 64), 64), :],
            a1s.at[i], a1r.at[i], device_id=(v, p), device_id_type=MESH)

    @pl.loop(1, GZ)
    def _(i):
        a2a1(i).start()

    own = pltpu.make_async_copy(S.at[g], T.at[:, pl.ds(pl.multiple_of(g * 64, 64), 64), :], lsem.at[0])
    own.start()
    own.wait()

    @pl.loop(1, GZ)
    def _(i):
        a2a1(i).wait()

    @pl.loop(0, 4)
    def _(p):
        blocks = [[T[r, pl.ds(2 * p + q, N, stride=8), :] for q in range(2)] for r in range(2)]
        rhs = jnp.concatenate([jnp.concatenate(b, axis=1) for b in blocks], axis=0)
        y = left(bhi[...], blo[...], rhs)
        kz = lax.broadcasted_iota(jnp.int32, (N, N), 0)
        kx = lax.broadcasted_iota(jnp.int32, (N, N), 1)
        qs = []
        for q in range(2):
            ky = g * 8 + 2 * p + q
            rest = (lax.rem(kz, 64) == 0) & (lax.rem(kx, 64) == 0) & (lax.rem(ky, 64) == 0)
            sq = s2col[...] + (s2row[...] + s2col[pl.ds(ky, 1), :])
            qs.append(jnp.where(rest, 0.0, (-1.0 / (N * N * N)) / jnp.where(rest, 1.0, sq)))
        qq = jnp.concatenate(qs, axis=1)
        y = jnp.concatenate([y[:N] * qq, y[N:] * qq], axis=0)
        y = left(ahi[...], alo[...], y)
        for r in range(2):
            for q in range(2):
                T2[r, pl.ds(2 * p + q, N, stride=8), :] = y[r * N:(r + 1) * N, q * N:(q + 1) * N]

    def a2a2(i):
        p = zpeer(i)
        return pltpu.make_async_remote_copy(
            T2.at[:, pl.ds(pl.multiple_of(p * 64, 64), 64), :], S2.at[g],
            a2s.at[i], a2r.at[i], device_id=(v, p), device_id_type=MESH)

    @pl.loop(1, GZ)
    def _(i):
        a2a2(i).start()

    own = pltpu.make_async_copy(T2.at[:, pl.ds(pl.multiple_of(g * 64, 64), 64), :], S2.at[g], lsem.at[1])
    own.start()
    own.wait()

    @pl.loop(1, GZ)
    def _(i):
        a2a2(i).wait()

    @pl.loop(0, LZ // 2)
    def _(p):
        blocks = []
        for r in range(2):
            blocks.append(jnp.concatenate(
                [S2[:, r, pl.ds(pl.multiple_of((2 * p + q) * 8, 8), 8), :].reshape(N, N) for q in range(2)], axis=1))
        y = left(ahi[...], alo[...], jnp.concatenate(blocks, axis=0))
        for q in range(2):
            c = jnp.concatenate([y[:N, q * N:(q + 1) * N], y[N:, q * N:(q + 1) * N]], axis=1)
            phi = right(c, bhi[...], blo[...])
            Pf[0, 2 * p + q + 1] = phi[:, :N]
            Pf[1, 2 * p + q + 1] = phi[:, N:]

    edge0 = pltpu.make_async_remote_copy(
        Pf.at[:, LZ:LZ + 1], Pf.at[:, 0:1], ps.at[0], pr.at[0], device_id=(v, nxt), device_id_type=MESH)
    edge1 = pltpu.make_async_remote_copy(
        Pf.at[:, 1:2], Pf.at[:, LZ + 1:LZ + 2], ps.at[1], pr.at[1], device_id=(v, prv), device_id_type=MESH)
    edge0.start()
    edge1.start()

    def correct(z):
        for s in range(2):
            phi = Pf[s, z + 1]
            grads = (up(phi, 1) - down(phi, 1), up(phi, 0) - down(phi, 0), Pf[s, z + 2] - Pf[s, z])
            for c in range(3):
                out = E[3 * s + c, z + 2] + time_step * (Rt[3 * s + c, z + 1] - grads[c] * half_inv)
                if s == 0:
                    BN[c, z] = out
                else:
                    V[pl.ds(pl.multiple_of((c * LZ + z) * N, N), N), :] = out

    @pl.loop(1, LZ - 1)
    def _(z):
        correct(z)

    edge0.wait()
    edge1.wait()

    @pl.loop(0, 2)
    def _(i):
        correct((LZ - 1) * i)

    def a2a3(i):
        p = vpeer(i)
        return pltpu.make_async_remote_copy(
            V.at[pl.ds(pl.multiple_of(p * ROWS, 8), ROWS)], R.at[pl.ds(pl.multiple_of(v * ROWS, 8), ROWS)],
            vs.at[i], vr.at[i], device_id=(p, g), device_id_type=MESH)

    @pl.loop(1, NV)
    def _(i):
        a2a3(i).start()

    mine = pl.multiple_of(v * ROWS, 8)
    own = pltpu.make_async_copy(V.at[pl.ds(mine, ROWS)], R.at[pl.ds(mine, ROWS)], lsem.at[0])
    own.start()

    y8 = pl.multiple_of((v // 2) * 8, 8)
    odd = lax.rem(v, 2) == 1

    @pl.loop(0, LZ)
    def _(z):
        for c in range(3):
            blk = BN[c, z, pl.ds(y8, 8), :]
            base_out[c, z] = jnp.where(odd, blk[4:8], blk[0:4])

    own.wait()

    @pl.loop(1, NV)
    def _(i):
        a2a3(i).wait()

    def gram_step(k, acc):
        cols = [R[pl.ds(8 * k + j, NV, stride=ROWS), :] for j in range(8)]
        x = jnp.concatenate(cols, axis=1)
        X[k] = x
        return acc + lax.dot_general(x, x, (((1,), (1,)), ((), ())), precision=lax.Precision.HIGHEST,
                                     preferred_element_type=f32)

    gram = lax.fori_loop(0, ROWS // 8, gram_step, jnp.zeros((NV, NV), f32))
    gbuf[...] = jnp.zeros((NV, N), f32)
    gbuf[:, 0:NV] = gram
    full = gbuf[...]
    packed = full[0:8]
    for b in range(1, 4):
        packed = packed + pltpu.roll(full[8 * b:8 * b + 8], 32 * b, 1)

    gsend[...] = packed
    grecv[g] = packed

    def ex1(i):
        return pltpu.make_async_remote_copy(
            gsend, grecv.at[g], gs.at[i], gr.at[i], device_id=(v, zpeer(i)), device_id_type=MESH)

    @pl.loop(1, GZ)
    def _(i):
        ex1(i).start()

    @pl.loop(1, GZ)
    def _(i):
        ex1(i).wait()

    total = grecv[0]
    for i in range(1, GZ):
        total = total + grecv[i]
    vsend[...] = total
    vrecv[v] = total

    def ex2(i):
        return pltpu.make_async_remote_copy(
            vsend, vrecv.at[v], ws.at[i], wr.at[i], device_id=(vpeer(i), g), device_id_type=MESH)

    @pl.loop(1, NV)
    def _(i):
        ex2(i).start()

    @pl.loop(1, NV)
    def _(i):
        ex2(i).wait()

    total = vrecv[0]
    for i in range(1, NV):
        total = total + vrecv[i]
    total = total / (3.0 * N * N * N)
    lane = lax.broadcasted_iota(jnp.int32, (NV, N), 1)
    row = lax.broadcasted_iota(jnp.int32, (NV, N), 0)
    m = jnp.concatenate([total] + [pltpu.roll(total, N - 32 * b, 1) for b in range(1, 4)], axis=0)
    m = jnp.where(lane < NV, m, jnp.where(lane == row + NV, 1.0, 0.0))
    for k in range(NV - 1):
        col = jnp.broadcast_to(m[:, k:k + 1], (NV, N))
        prow = m[k:k + 1, :]
        piv = col[k:k + 1, :]
        fac = jnp.where(row > k, col * (1.0 / piv), 0.0)
        m = m - fac * prow
    diag = jnp.where(lane == row, m, 0.0)
    dcol = jnp.sum(diag, axis=1, keepdims=True)
    drow = jnp.sum(diag, axis=0, keepdims=True)
    growth[...] = 0.5 * jnp.log(drow[:, 0:NV])
    inv = pltpu.roll(m, N - NV, 1) * (1.0 / jnp.sqrt(dcol))
    inv = inv[:, 0:NV]

    @pl.loop(0, ROWS // 8)
    def _(k):
        o = lax.dot_general(inv, X[k], (((1,), (0,)), ((), ())), precision=lax.Precision.HIGHEST,
                            preferred_element_type=f32)
        for j in range(8):
            O2[pl.ds(8 * k + j, NV, stride=ROWS), :] = o[:, j * N:(j + 1) * N]

    def a2a4(i):
        p = vpeer(i)
        return pltpu.make_async_remote_copy(
            O2.at[pl.ds(pl.multiple_of(p * ROWS, 8), ROWS)], ortho.at[pl.ds(pl.multiple_of(v * ROWS, 8), ROWS)],
            os_.at[i], or_.at[i], device_id=(p, g), device_id_type=MESH)

    @pl.loop(1, NV)
    def _(i):
        a2a4(i).start()

    own = pltpu.make_async_copy(O2.at[pl.ds(mine, ROWS)], ortho.at[pl.ds(mine, ROWS)], lsem.at[1])
    own.start()
    own.wait()

    @pl.loop(1, NV)
    def _(i):
        a2a4(i).wait()


def per_device(base_flow, tangents, shells):
    ahi, alo, bhi, blo, sine, slope2 = tables()
    vm = pl.BlockSpec(memory_space=pltpu.VMEM)
    sm = pl.BlockSpec(memory_space=pltpu.SMEM)
    anyspace = pl.BlockSpec(memory_space=pl.ANY)
    dma = pltpu.SemaphoreType.DMA
    plane = (N, N)
    base_rows, ortho, growth = pl.pallas_call(
        kernel,
        out_shape=(
            jax.ShapeDtypeStruct((3, LZ, N // NV, N), f32),
            jax.ShapeDtypeStruct((3 * LZ * N, N), f32),
            jax.ShapeDtypeStruct((1, NV), f32),
        ),
        in_specs=[sm, sm, anyspace, anyspace, vm, vm, vm, vm, vm, vm],
        out_specs=(vm, anyspace, vm),
        scratch_shapes=[
            pltpu.VMEM((6, 12) + plane, f32),
            pltpu.VMEM((6, 10) + plane, f32),
            pltpu.VMEM((GZ, 2, 64, N), f32),
            pltpu.VMEM((2, 1024, N), f32),
            pltpu.VMEM((2, 1024, N), f32),
            pltpu.VMEM((GZ, 2, 64, N), f32),
            pltpu.VMEM((2, LZ + 2) + plane, f32),
            pltpu.VMEM((3 * LZ * N, N), f32),
            pltpu.VMEM((3, LZ) + plane, f32),
            pltpu.VMEM((3 * LZ * N, N), f32),
            pltpu.VMEM((ROWS // 8, NV, 8 * N), f32),
            pltpu.VMEM((3 * LZ * N, N), f32),
            pltpu.VMEM((NV, N), f32),
            pltpu.VMEM((8, N), f32),
            pltpu.VMEM((GZ, 8, N), f32),
            pltpu.VMEM((8, N), f32),
            pltpu.VMEM((NV, 8, N), f32),
            dma((2,)),
            dma((8,)), dma((8,)),
            dma((GZ,)), dma((GZ,)),
            dma((GZ,)), dma((GZ,)),
            dma((2,)), dma((2,)),
            dma((NV,)), dma((NV,)),
            dma((GZ,)), dma((GZ,)),
            dma((NV,)), dma((NV,)),
            dma((NV,)), dma((NV,)),
        ],
        compiler_params=pltpu.CompilerParams(
            collective_id=0, has_side_effects=True, vmem_limit_bytes=58 * 1024 * 1024
        ),
    )(
        shells, jnp.asarray(sine), base_flow, tangents[0],
        jnp.asarray(ahi), jnp.asarray(alo), jnp.asarray(bhi), jnp.asarray(blo),
        jnp.broadcast_to(jnp.asarray(slope2)[None, :], (1, N)),
        jnp.broadcast_to(jnp.asarray(slope2)[:, None], (N, N)),
    )
    return base_rows, ortho.reshape(tangents.shape), growth[0]


def solution(mesh):
    in_specs = (P(None, "gz", None, None), P("vec", None, "gz", None, None), P())
    out_specs = (P(None, "gz", "vec", None), P("vec", None, "gz", None, None), P())
    return jax.shard_map(
        per_device, mesh=mesh, in_specs=in_specs, out_specs=out_specs, check_vma=False
    )
```

time: 692 us -> 248 us (0.36)
  the two profiles are of different devices: /device:TPU:32 before, /device:TPU:1 now
where the time goes in v1:
time: 248 us; the launch traced here: 247 us
  Pallas kernels  241 us (97%)
  local copies, waits for them, and re-layouts  6.01 us (2%)
    pallas_call x1, Pallas kernels, per_device(): pl.pallas_call(kernel, out_shape=(jax.ShapeDtypeStruct((3, LZ, N // NV, N...  241 us

profile of v1, /device:TPU:1, one launch (start us, length us, event | category | flops | bytes accessed | tf_op | source)
XLA Modules:
  0.0 247.4 jit_solution(6023600530772822681)
XLA Ops:
  0.6 1.4 broadcast_in_dim.10.s2col
  2.0 240.8 %shard_map.112 = (f32[3,8,4,128]{3,2,1,0:T(4,128)}, f32[3072,128]{1,0:T(8,128)}, f32[1,32]{1,0:T(1,128)}) custom-call(s32[4]{0:T(128)} %shells.1, f32[128]{0:T(128)} %constant.12.clone.sine, f32[3,8,128,128]{3,2,1,0:T(8,128)} %base.1, f32[3,8,128,128]{3,2,1,0:T(8,128)} %bitcast.3, bf16[256,256]{1,0:T(8,128)(2,1)} %constant.13.clone.ahi, ...), custom_call_target="tpu_custom_call" | custom-call | tf_op jit(solution)/shard_map/pallas_call | solution.py:403
  242.8 1.4 copy.15
  244.2 0.0 copy-start
  244.2 2.7 %copy.16 = f32[1,3,8,128,128]{4,3,2,1,0:T(8,128)} copy(f32[1,3,8,128,128]{4,3,2,1,0:T(8,128)} %bitcast.4) | data formatting | bytes 3145728
  246.9 0.0 copy-done
  246.9 0.5 copy.17
Async XLA Ops:
  244.2 2.7 %copy-start = (f32[1,32]{1,0:T(1,128)S(1)}, f32[1,32]{1,0:T(1,128)}, u32[]{:S(2)}) copy-start(f32[1,32]{1,0:T(1,128)} %get-tuple-element.8) | copy-start | bytes 388

commit v2 on v1

--- a/solution.py
+++ b/solution.py
@@ -66,18 +66,21 @@
 
 def kernel(shells, sine, base, tang, ahi, alo, bhi, blo, s2row, s2col,
            base_out, ortho, growth,
-           E, Rt, S, T, T2, S2, Pf, V, BN, R, X, O2, gbuf, gsend, grecv, vsend, vrecv,
-           lsem, hs, hr, a1s, a1r, a2s, a2r, ps, pr, vs, vr, gs, gr, ws, wr, os_, or_):
+           E, Rt, S, T, T2, S2, Pf, YS, BN, R, PS, RE, hsend, hrecv, HB, V2, X, O2, O5, gbuf, gsend, grecv, vsend, vrecv,
+           lsem, hs, hr, a1s, a1r, a2s, a2r, ps, pr, ys, yr, es, er, fs, fr, ns, nr, gs, gr, ws, wr, os_, or_):
     v = lax.axis_index("vec")
     g = lax.axis_index("gz")
     nxt = lax.rem(g + 1, GZ)
     prv = lax.rem(g + GZ - 1, GZ)
+    half = v // 16
+    ring = lax.rem(v, 16)
+    other = (1 - half) * 16 + ring
 
     def zpeer(i):
         return lax.rem(g + i, GZ)
 
     def vpeer(i):
-        return lax.rem(v + i, NV)
+        return lax.rem(half + i // 16, 2) * 16 + lax.rem(ring + i, 16)
 
     barrier = pltpu.get_barrier_semaphore()
 
@@ -88,26 +91,16 @@
     @pl.loop(1, NV)
     def _(i):
         pl.semaphore_signal(barrier, inc=1, device_id=(vpeer(i), g), device_id_type=MESH)
+
+    above = (other, lax.rem(g + half, GZ))
+    below = (other, lax.rem(g + GZ - 1 + half, GZ))
+    diagonal = (other, lax.rem(g + GZ - 1 + 2 * half, GZ))
+    pl.semaphore_signal(barrier, inc=1, device_id=diagonal, device_id_type=MESH)
 
     load0 = pltpu.make_async_copy(base, E.at[0:3, 2:10], lsem.at[0])
     load1 = pltpu.make_async_copy(tang, E.at[3:6, 2:10], lsem.at[1])
     load0.start()
     load1.start()
-    pl.semaphore_wait(barrier, GZ + NV - 2)
-
-    halos = []
-    for f, src in ((0, base), (3, tang)):
-        for who, a, b in ((nxt, (LZ - 1, LZ - 2), (1, 0)), (prv, (0, 0), (10, 10))):
-            n = len(halos)
-            halos.append(pltpu.make_async_remote_copy(
-                src.at[0:2, a[0]:a[0] + 1], E.at[f:f + 2, b[0]:b[0] + 1],
-                hs.at[n], hr.at[n], device_id=(v, who), device_id_type=MESH))
-            n += 1
-            halos.append(pltpu.make_async_remote_copy(
-                src.at[2, a[1]:a[1] + 2], E.at[f + 2, b[1]:b[1] + 2],
-                hs.at[n], hr.at[n], device_id=(v, who), device_id_type=MESH))
-    for h in halos:
-        h.start()
     load0.wait()
     load1.wait()
 
@@ -118,8 +111,6 @@
             f = E[c, e]
             xp, xm, yp, ym, zp, zm = up(f, 1), down(f, 1), up(f, 0), down(f, 0), E[c, e + 1], E[c, e - 1]
             dx, dy, dz = xp - xm, yp - ym, zp - zm
-            if comps != (2,):
-                pass
             lap = ((xp + xm) + (yp + ym)) + (zp + zm) - 6.0 * f
             brate = lap * lap_scale - (bx * dx + by * dy + bz * dz) * half_inv
             if c == 0:
@@ -134,11 +125,49 @@
             xp, xm, yp, ym, zp, zm = up(f, 1), down(f, 1), up(f, 0), down(f, 0), E[c + 3, e + 1], E[c + 3, e - 1]
             lap = ((xp + xm) + (yp + ym)) + (zp + zm) - 6.0 * f
             adv = adv + (bx * (xp - xm) + by * (yp - ym) + bz * (zp - zm))
-            Rt[c + 3, e - 1] = lap * lap_scale - adv * half_inv
+            trate = lap * lap_scale - adv * half_inv
+            Rt[c + 3, e - 1] = trate
+            if len(comps) == 3:
+                z = e - 2
+                YS[pl.ds((z // 4) * 16, 16), c, lax.rem(z, 4)] = (f + time_step * trate).reshape(16, 8, N)
 
     @pl.loop(3, 9)
     def _(e):
         rates(e, (0, 1, 2))
+
+    pl.semaphore_wait(barrier, GZ + NV - 1)
+
+    halos = []
+    for f, src in ((3, tang), (0, base)):
+        for who, a, b in ((nxt, (LZ - 1, LZ - 2), (1, 0)), (prv, (0, 0), (10, 10))):
+            n = len(halos)
+            halos.append(pltpu.make_async_remote_copy(
+                src.at[0:2, a[0]:a[0] + 1], E.at[f:f + 2, b[0]:b[0] + 1],
+                hs.at[n], hr.at[n], device_id=(v, who), device_id_type=MESH))
+            n += 1
+            halos.append(pltpu.make_async_remote_copy(
+                src.at[2, a[1]:a[1] + 2], E.at[f + 2, b[1]:b[1] + 2],
+                hs.at[n], hr.at[n], device_id=(v, who), device_id_type=MESH))
+    for h in halos:
+        h.start()
+
+    def inner(i):
+        p = vpeer(i)
+        z = 1 - p // 16
+        return pltpu.make_async_remote_copy(
+            YS.at[p, :, pl.ds(z, 3)], R.at[v, :, pl.ds(z, 3)],
+            ys.at[i], yr.at[i], device_id=(p, g), device_id_type=MESH)
+
+    def outer(i):
+        p = vpeer(i)
+        z = 3 * (p // 16)
+        return pltpu.make_async_remote_copy(
+            YS.at[p, :, z], R.at[v, :, z],
+            es.at[i], er.at[i], device_id=(p, g), device_id_type=MESH)
+
+    @pl.loop(1, NV)
+    def _(i):
+        inner(i).start()
 
     for h in halos:
         h.wait()
@@ -181,6 +210,12 @@
     def _(i):
         a2a1(i).start()
 
+    @pl.loop(1, NV)
+    def _(i):
+        outer(i).start()
+
+    keep = pltpu.make_async_copy(YS.at[v], R.at[v], lsem.at[2])
+    keep.start()
     own = pltpu.make_async_copy(S.at[g], T.at[:, pl.ds(pl.multiple_of(g * 64, 64), 64), :], lsem.at[0])
     own.start()
     own.wait()
@@ -237,69 +272,97 @@
         for q in range(2):
             c = jnp.concatenate([y[:N, q * N:(q + 1) * N], y[N:, q * N:(q + 1) * N]], axis=1)
             phi = right(c, bhi[...], blo[...])
-            Pf[0, 2 * p + q + 1] = phi[:, :N]
-            Pf[1, 2 * p + q + 1] = phi[:, N:]
-
+            z = 2 * p + q
+            Pf[z + 1] = phi[:, :N]
+            PS[pl.ds((z // 4) * 16, 16), lax.rem(z, 4)] = phi[:, N:].reshape(16, 8, N)
+
+    def phis(i):
+        p = vpeer(i)
+        return pltpu.make_async_remote_copy(
+            PS.at[p], RE.at[v, 1:5], fs.at[i], fr.at[i], device_id=(p, g), device_id_type=MESH)
+
+    @pl.loop(1, NV)
+    def _(i):
+        phis(i).start()
+
+    mine = pltpu.make_async_copy(PS.at[v], RE.at[v, 1:5], lsem.at[0])
+    mine.start()
+
+    y8 = pl.multiple_of((v // 2) * 8, 8)
+    odd = lax.rem(v, 2) == 1
     edge0 = pltpu.make_async_remote_copy(
-        Pf.at[:, LZ:LZ + 1], Pf.at[:, 0:1], ps.at[0], pr.at[0], device_id=(v, nxt), device_id_type=MESH)
+        Pf.at[LZ, pl.ds(y8, 8)], Pf.at[0, pl.ds(y8, 8)], ps.at[0], pr.at[0], device_id=(v, nxt), device_id_type=MESH)
     edge1 = pltpu.make_async_remote_copy(
-        Pf.at[:, 1:2], Pf.at[:, LZ + 1:LZ + 2], ps.at[1], pr.at[1], device_id=(v, prv), device_id_type=MESH)
+        Pf.at[1, pl.ds(y8, 8)], Pf.at[LZ + 1, pl.ds(y8, 8)], ps.at[1], pr.at[1], device_id=(v, prv), device_id_type=MESH)
     edge0.start()
     edge1.start()
 
-    def correct(z):
-        for s in range(2):
-            phi = Pf[s, z + 1]
-            grads = (up(phi, 1) - down(phi, 1), up(phi, 0) - down(phi, 0), Pf[s, z + 2] - Pf[s, z])
-            for c in range(3):
-                out = E[3 * s + c, z + 2] + time_step * (Rt[3 * s + c, z + 1] - grads[c] * half_inv)
-                if s == 0:
-                    BN[c, z] = out
-                else:
-                    V[pl.ds(pl.multiple_of((c * LZ + z) * N, N), N), :] = out
-
-    @pl.loop(1, LZ - 1)
+    @pl.loop(0, LZ)
     def _(z):
-        correct(z)
+        phi = Pf[z + 1]
+        BN[0, z] = up(phi, 1) - down(phi, 1)
+        BN[1, z] = up(phi, 0) - down(phi, 0)
 
     edge0.wait()
     edge1.wait()
 
-    @pl.loop(0, 2)
-    def _(i):
-        correct((LZ - 1) * i)
-
-    def a2a3(i):
-        p = vpeer(i)
-        return pltpu.make_async_remote_copy(
-            V.at[pl.ds(pl.multiple_of(p * ROWS, 8), ROWS)], R.at[pl.ds(pl.multiple_of(v * ROWS, 8), ROWS)],
-            vs.at[i], vr.at[i], device_id=(p, g), device_id_type=MESH)
-
-    @pl.loop(1, NV)
-    def _(i):
-        a2a3(i).start()
-
-    mine = pl.multiple_of(v * ROWS, 8)
-    own = pltpu.make_async_copy(V.at[pl.ds(mine, ROWS)], R.at[pl.ds(mine, ROWS)], lsem.at[0])
-    own.start()
-
-    y8 = pl.multiple_of((v // 2) * 8, 8)
-    odd = lax.rem(v, 2) == 1
-
     @pl.loop(0, LZ)
     def _(z):
+        rows = pl.ds(y8, 8)
+        grads = (BN[0, z, rows], BN[1, z, rows], Pf[z + 2, rows] - Pf[z, rows])
         for c in range(3):
-            blk = BN[c, z, pl.ds(y8, 8), :]
+            blk = E[c, z + 2, rows] + time_step * (Rt[c, z + 1, rows] - grads[c] * half_inv)
             base_out[c, z] = jnp.where(odd, blk[4:8], blk[0:4])
 
-    own.wait()
-
-    @pl.loop(1, NV)
-    def _(i):
-        a2a3(i).wait()
+    mine.wait()
+
+    @pl.loop(1, NV)
+    def _(i):
+        phis(i).wait()
+
+    for z in range(4):
+        hsend[0, z * NV:(z + 1) * NV] = RE[:, z + 1, 7, :]
+        hsend[1, z * NV:(z + 1) * NV] = RE[:, z + 1, 0, :]
+    rimhi = half * 16 + lax.rem(ring + 1, 16)
+    rimlo = half * 16 + lax.rem(ring + 15, 16)
+    rims = [
+        pltpu.make_async_remote_copy(hsend.at[0], hrecv.at[0], ns.at[0], nr.at[0], device_id=(rimhi, g), device_id_type=MESH),
+        pltpu.make_async_remote_copy(hsend.at[1], hrecv.at[1], ns.at[1], nr.at[1], device_id=(rimlo, g), device_id_type=MESH),
+        pltpu.make_async_remote_copy(RE.at[:, 4], RE.at[:, 0], ns.at[2], nr.at[2], device_id=above, device_id_type=MESH),
+        pltpu.make_async_remote_copy(RE.at[:, 1], RE.at[:, 5], ns.at[3], nr.at[3], device_id=below, device_id_type=MESH),
+    ]
+    for c in rims:
+        c.start()
+    keep.wait()
+
+    @pl.loop(1, NV)
+    def _(i):
+        inner(i).wait()
+
+    @pl.loop(1, NV)
+    def _(i):
+        outer(i).wait()
+
+    for c in rims:
+        c.wait()
+    HB[pl.ds(0, N, stride=8), :] = hrecv[0]
+    HB[pl.ds(7, N, stride=8), :] = hrecv[1]
+    sub = lax.broadcasted_iota(jnp.int32, (8, N), 0)
+
+    @pl.loop(0, NV)
+    def _(j):
+        for z in range(4):
+            phi = RE[j, z + 1]
+            rim = HB[pl.ds(pl.multiple_of((z * NV + j) * 8, 8), 8), :]
+            yp = jnp.where(sub == 7, rim, pltpu.roll(phi, 7, 0))
+            ym = jnp.where(sub == 0, rim, pltpu.roll(phi, 1, 0))
+            grads = (up(phi, 1) - down(phi, 1), yp - ym, RE[j, z + 2] - RE[j, z])
+            for c in range(3):
+                V2[pl.ds(pl.multiple_of(j * ROWS + c * 32 + z * 8, 8), 8), :] = (
+                    R[j, c, z] - (time_step * half_inv) * grads[c])
 
     def gram_step(k, acc):
-        cols = [R[pl.ds(8 * k + j, NV, stride=ROWS), :] for j in range(8)]
+        cols = [V2[pl.ds(8 * k + j, NV, stride=ROWS), :] for j in range(8)]
         x = jnp.concatenate(cols, axis=1)
         X[k] = x
         return acc + lax.dot_general(x, x, (((1,), (1,)), ((), ())), precision=lax.Precision.HIGHEST,
@@ -374,17 +437,23 @@
         for j in range(8):
             O2[pl.ds(8 * k + j, NV, stride=ROWS), :] = o[:, j * N:(j + 1) * N]
 
+    @pl.loop(0, NV)
+    def _(i):
+        for c in range(3):
+            for z in range(4):
+                O5[i, c, z] = O2[pl.ds(pl.multiple_of(i * ROWS + c * 32 + z * 8, 8), 8), :]
+
     def a2a4(i):
         p = vpeer(i)
         return pltpu.make_async_remote_copy(
-            O2.at[pl.ds(pl.multiple_of(p * ROWS, 8), ROWS)], ortho.at[pl.ds(pl.multiple_of(v * ROWS, 8), ROWS)],
+            O5.at[p], ortho.at[:, pl.ds(half * 4, 4), ring],
             os_.at[i], or_.at[i], device_id=(p, g), device_id_type=MESH)
 
     @pl.loop(1, NV)
     def _(i):
         a2a4(i).start()
 
-    own = pltpu.make_async_copy(O2.at[pl.ds(mine, ROWS)], ortho.at[pl.ds(mine, ROWS)], lsem.at[1])
+    own = pltpu.make_async_copy(O5.at[v], ortho.at[:, pl.ds(half * 4, 4), ring], lsem.at[1])
     own.start()
     own.wait()
 
@@ -404,7 +473,7 @@
         kernel,
         out_shape=(
             jax.ShapeDtypeStruct((3, LZ, N // NV, N), f32),
-            jax.ShapeDtypeStruct((3 * LZ * N, N), f32),
+            jax.ShapeDtypeStruct((3, LZ, 16, 8, N), f32),
             jax.ShapeDtypeStruct((1, NV), f32),
         ),
         in_specs=[sm, sm, anyspace, anyspace, vm, vm, vm, vm, vm, vm],
@@ -416,23 +485,33 @@
             pltpu.VMEM((2, 1024, N), f32),
             pltpu.VMEM((2, 1024, N), f32),
             pltpu.VMEM((GZ, 2, 64, N), f32),
-            pltpu.VMEM((2, LZ + 2) + plane, f32),
-            pltpu.VMEM((3 * LZ * N, N), f32),
-            pltpu.VMEM((3, LZ) + plane, f32),
+            pltpu.VMEM((LZ + 2,) + plane, f32),
+            pltpu.VMEM((NV, 3, 4, 8, N), f32),
+            pltpu.VMEM((2, LZ) + plane, f32),
+            pltpu.VMEM((NV, 3, 4, 8, N), f32),
+            pltpu.VMEM((NV, 4, 8, N), f32),
+            pltpu.VMEM((NV, 6, 8, N), f32),
+            pltpu.VMEM((2,) + plane, f32),
+            pltpu.VMEM((2,) + plane, f32),
+            pltpu.VMEM((8 * N, N), f32),
             pltpu.VMEM((3 * LZ * N, N), f32),
             pltpu.VMEM((ROWS // 8, NV, 8 * N), f32),
             pltpu.VMEM((3 * LZ * N, N), f32),
+            pltpu.VMEM((NV, 3, 4, 8, N), f32),
             pltpu.VMEM((NV, N), f32),
             pltpu.VMEM((8, N), f32),
             pltpu.VMEM((GZ, 8, N), f32),
             pltpu.VMEM((8, N), f32),
             pltpu.VMEM((NV, 8, N), f32),
-            dma((2,)),
+            dma((3,)),
             dma((8,)), dma((8,)),
             dma((GZ,)), dma((GZ,)),
             dma((GZ,)), dma((GZ,)),
             dma((2,)), dma((2,)),
             dma((NV,)), dma((NV,)),
+            dma((NV,)), dma((NV,)),
+            dma((NV,)), dma((NV,)),
+            dma((4,)), dma((4,)),
             dma((GZ,)), dma((GZ,)),
             dma((NV,)), dma((NV,)),
             dma((NV,)), dma((NV,)),
@@ -443,8 +522,8 @@
     )(
         shells, jnp.asarray(sine), base_flow, tangents[0],
         jnp.asarray(ahi), jnp.asarray(alo), jnp.asarray(bhi), jnp.asarray(blo),
-        jnp.broadcast_to(jnp.asarray(slope2)[None, :], (1, N)),
-        jnp.broadcast_to(jnp.asarray(slope2)[:, None], (N, N)),
+        jnp.asarray(slope2[None, :]),
+        jnp.asarray(np.repeat(slope2[:, None], N, axis=1)),
     )
     return base_rows, ortho.reshape(tangents.shape), growth[0]
 

time: 248 us -> 228 us (0.919)
  Pallas kernels: 241 us -> 222 us
    pallas_call x1, Pallas kernels: 241 us -> 222 us  [per_device(): pl.pallas_call(kernel, out_shape=(jax.ShapeDtypeStruct((3, LZ, N // NV, N...]
where the time goes in v2:
time: 228 us
  Pallas kernels  222 us (97%)
  local copies, waits for them, and re-layouts  4.64 us (2%)
    pallas_call x1, Pallas kernels, per_device(): pl.pallas_call(kernel, out_shape=(jax.ShapeDtypeStruct((3, LZ, N // NV, N...  222 us
    unnamed x5, local copies, waits for them, and re-layouts  4.64 us

profile of v2, /device:TPU:1, one launch (start us, length us, event | category | flops | bytes accessed | tf_op | source)
XLA Modules:
  0.0 227.7 jit_solution(7645646412018071071)
XLA Ops:
  0.6 222.4 %shard_map.121 = (f32[3,8,4,128]{3,2,1,0:T(4,128)}, f32[3,8,16,8,128]{4,3,2,1,0:T(8,128)}, f32[1,32]{1,0:T(1,128)}) custom-call(s32[4]{0:T(128)} %shells.1, f32[128]{0:T(128)} %constant.14.clone.sine, f32[3,8,128,128]{3,2,1,0:T(8,128)} %base.1, f32[3,8,128,128]{3,2,1,0:T(8,128)} %bitcast.3, bf16[256,256]{1,0:T(8,128)(2,1)} %constant.15.clone.ahi, ...), custom_call_target="tpu_custom_call" | custom-call | tf_op jit(solution)/shard_map/pallas_call | solution.py:472
  223.0 1.4 copy.16
  224.4 0.0 copy-start
  224.4 2.7 %copy.17 = f32[1,3,8,128,128]{4,3,2,1,0:T(8,128)} copy(f32[1,3,8,128,128]{4,3,2,1,0:T(8,128)} %bitcast.4) | data formatting | bytes 3145728
  227.2 0.0 copy-done
  227.2 0.5 copy.18
Async XLA Ops:
  224.4 2.7 %copy-start = (f32[1,32]{1,0:T(1,128)S(1)}, f32[1,32]{1,0:T(1,128)}, u32[]{:S(2)}) copy-start(f32[1,32]{1,0:T(1,128)} %get-tuple-element.8) | copy-start | bytes 388

commit v3 on v2

--- a/solution.py
+++ b/solution.py
@@ -34,7 +34,11 @@
     sine = np.sin(2.0 * np.pi / N * k)
     sine[[0, 64]] = 0.0
     slope2 = ((sine / spacing) ** 2).astype(np.float32)
-    return hi, lo, np.ascontiguousarray(hi.T), np.ascontiguousarray(lo.T), sine.astype(np.float32), slope2
+    lines = np.zeros((N + 16, N), np.float32)
+    lines[:N] = slope2[:, None]
+    lines[N] = slope2
+    lines[N + 8] = sine
+    return np.stack([hi, lo, hi.T, lo.T]), lines
 
 
 def split(x):
@@ -64,10 +68,10 @@
     return pltpu.roll(x, 1, axis)
 
 
-def kernel(shells, sine, base, tang, ahi, alo, bhi, blo, s2row, s2col,
+def kernel(shells_in, base, tang, dft_in, lines_in,
            base_out, ortho, growth,
-           E, Rt, S, T, T2, S2, Pf, YS, BN, R, PS, RE, hsend, hrecv, HB, V2, X, O2, O5, gbuf, gsend, grecv, vsend, vrecv,
-           lsem, hs, hr, a1s, a1r, a2s, a2r, ps, pr, ys, yr, es, er, fs, fr, ns, nr, gs, gr, ws, wr, os_, or_):
+           shells, dft, lines, E, Rt, S, T, T2, S2, Pf, YS, BN, R, PS, RE, hsend, hrecv, HB, V2, X, O5, gbuf, gsend, grecv, vsend, vrecv,
+           lsem, hs, hr, a1s, a1r, a2s, a2r, ps, pr, xs, xr, ys, yr, es, er, fs, fr, f2s, f2r, ns, nr, gs, gr, ws, wr, os_, or_):
     v = lax.axis_index("vec")
     g = lax.axis_index("gz")
     nxt = lax.rem(g + 1, GZ)
@@ -82,27 +86,49 @@
     def vpeer(i):
         return lax.rem(half + i // 16, 2) * 16 + lax.rem(ring + i, 16)
 
+    def landed(src, dst, sent, received):
+        every = pltpu.make_async_remote_copy(
+            src, dst, sent, received, device_id=(vpeer(1), g), device_id_type=MESH)
+        every.wait_send()
+        every.wait_recv()
+
     barrier = pltpu.get_barrier_semaphore()
 
+    def far(t):
+        u = t // 2
+        d = lax.rem(8 + ((u + 1) // 2) * (2 * lax.rem(u, 2) - 1), 16)
+        return (1 - lax.rem(t, 2)) * 16 + d
+
+    @pl.loop(0, NV - 1)
+    def _(t):
+        pl.semaphore_signal(barrier, inc=1, device_id=(vpeer(far(t)), g), device_id_type=MESH)
+
     @pl.loop(1, GZ)
     def _(i):
         pl.semaphore_signal(barrier, inc=1, device_id=(v, zpeer(i)), device_id_type=MESH)
-
-    @pl.loop(1, NV)
-    def _(i):
-        pl.semaphore_signal(barrier, inc=1, device_id=(vpeer(i), g), device_id_type=MESH)
 
     above = (other, lax.rem(g + half, GZ))
     below = (other, lax.rem(g + GZ - 1 + half, GZ))
     diagonal = (other, lax.rem(g + GZ - 1 + 2 * half, GZ))
     pl.semaphore_signal(barrier, inc=1, device_id=diagonal, device_id_type=MESH)
 
+    load2 = pltpu.make_async_copy(shells_in, shells, lsem.at[2])
+    load2.start()
     load0 = pltpu.make_async_copy(base, E.at[0:3, 2:10], lsem.at[0])
     load1 = pltpu.make_async_copy(tang, E.at[3:6, 2:10], lsem.at[1])
     load0.start()
     load1.start()
+    load3 = pltpu.make_async_copy(lines_in, lines, lsem.at[3])
+    load4 = pltpu.make_async_copy(dft_in, dft, lsem.at[4])
+    load3.start()
+    load4.start()
+    load2.wait()
+    load3.wait()
     load0.wait()
     load1.wait()
+    sine = lines[N + 8:N + 9, :]
+    laneid = lax.broadcasted_iota(jnp.int32, (1, N), 1)
+    ahi, alo, bhi, blo = dft.at[0], dft.at[1], dft.at[2], dft.at[3]
 
     def rates(e, comps):
         bx, by, bz = E[0, e], E[1, e], E[2, e]
@@ -115,10 +141,10 @@
             brate = lap * lap_scale - (bx * dx + by * dy + bz * dz) * half_inv
             if c == 0:
                 zz = g * LZ + (e - 2)
-                prof = 0.0
+                picks = jnp.zeros((1, N), f32)
                 for j in range(4):
-                    prof = prof + sine[lax.rem(shells[j] * zz, N)]
-                brate = brate + prof * forcing_amplitude
+                    picks = picks + jnp.where(laneid == lax.rem(shells[j] * zz, N), sine, 0.0)
+                brate = brate + jnp.sum(picks, axis=1, keepdims=True) * forcing_amplitude
             Rt[c, e - 1] = brate
             adv = tx * dx + ty * dy + tz * dz
             f = E[c + 3, e]
@@ -131,9 +157,9 @@
                 z = e - 2
                 YS[pl.ds((z // 4) * 16, 16), c, lax.rem(z, 4)] = (f + time_step * trate).reshape(16, 8, N)
 
-    @pl.loop(3, 9)
-    def _(e):
-        rates(e, (0, 1, 2))
+    @pl.loop(0, 2)
+    def _(i):
+        rates(3 + 3 * i, (0, 1, 2))
 
     pl.semaphore_wait(barrier, GZ + NV - 1)
 
@@ -151,19 +177,32 @@
     for h in halos:
         h.start()
 
+    def first(i):
+        p = vpeer(i)
+        z = 1 - p // 16
+        return pltpu.make_async_remote_copy(
+            YS.at[p, :, z], R.at[v, :, z], xs, xr, device_id=(p, g), device_id_type=MESH)
+
     def inner(i):
         p = vpeer(i)
-        z = 1 - p // 16
-        return pltpu.make_async_remote_copy(
-            YS.at[p, :, pl.ds(z, 3)], R.at[v, :, pl.ds(z, 3)],
-            ys.at[i], yr.at[i], device_id=(p, g), device_id_type=MESH)
+        z = 2 - p // 16
+        return pltpu.make_async_remote_copy(
+            YS.at[p, :, pl.ds(z, 2)], R.at[v, :, pl.ds(z, 2)],
+            ys, yr, device_id=(p, g), device_id_type=MESH)
 
     def outer(i):
         p = vpeer(i)
         z = 3 * (p // 16)
         return pltpu.make_async_remote_copy(
-            YS.at[p, :, z], R.at[v, :, z],
-            es.at[i], er.at[i], device_id=(p, g), device_id_type=MESH)
+            YS.at[p, :, z], R.at[v, :, z], es, er, device_id=(p, g), device_id_type=MESH)
+
+    @pl.loop(1, NV)
+    def _(i):
+        first(i).start()
+
+    @pl.loop(0, 4)
+    def _(i):
+        rates(4 + i + i // 2, (0, 1, 2))
 
     @pl.loop(1, NV)
     def _(i):
@@ -179,6 +218,8 @@
     @pl.loop(0, 2)
     def _(i):
         rates(1 + 9 * i, (2,))
+
+    load4.wait()
 
     @pl.loop(0, LZ // 2)
     def _(p):
@@ -204,7 +245,7 @@
         p = zpeer(i)
         return pltpu.make_async_remote_copy(
             S.at[p], T.at[:, pl.ds(pl.multiple_of(g * 64, 64), 64), :],
-            a1s.at[i], a1r.at[i], device_id=(v, p), device_id_type=MESH)
+            a1s, a1r, device_id=(v, p), device_id_type=MESH)
 
     @pl.loop(1, GZ)
     def _(i):
@@ -214,15 +255,13 @@
     def _(i):
         outer(i).start()
 
-    keep = pltpu.make_async_copy(YS.at[v], R.at[v], lsem.at[2])
+    keep = pltpu.make_async_copy(YS.at[v], R.at[v], lsem.at[5])
     keep.start()
     own = pltpu.make_async_copy(S.at[g], T.at[:, pl.ds(pl.multiple_of(g * 64, 64), 64), :], lsem.at[0])
     own.start()
     own.wait()
 
-    @pl.loop(1, GZ)
-    def _(i):
-        a2a1(i).wait()
+    landed(S.at[0:GZ - 1], T.at[:, 0:64 * (GZ - 1)], a1s, a1r)
 
     @pl.loop(0, 4)
     def _(p):
@@ -235,7 +274,7 @@
         for q in range(2):
             ky = g * 8 + 2 * p + q
             rest = (lax.rem(kz, 64) == 0) & (lax.rem(kx, 64) == 0) & (lax.rem(ky, 64) == 0)
-            sq = s2col[...] + (s2row[...] + s2col[pl.ds(ky, 1), :])
+            sq = lines[0:N, :] + (lines[N:N + 1, :] + lines[pl.ds(ky, 1), :])
             qs.append(jnp.where(rest, 0.0, (-1.0 / (N * N * N)) / jnp.where(rest, 1.0, sq)))
         qq = jnp.concatenate(qs, axis=1)
         y = jnp.concatenate([y[:N] * qq, y[N:] * qq], axis=0)
@@ -248,7 +287,7 @@
         p = zpeer(i)
         return pltpu.make_async_remote_copy(
             T2.at[:, pl.ds(pl.multiple_of(p * 64, 64), 64), :], S2.at[g],
-            a2s.at[i], a2r.at[i], device_id=(v, p), device_id_type=MESH)
+            a2s, a2r, device_id=(v, p), device_id_type=MESH)
 
     @pl.loop(1, GZ)
     def _(i):
@@ -258,9 +297,7 @@
     own.start()
     own.wait()
 
-    @pl.loop(1, GZ)
-    def _(i):
-        a2a2(i).wait()
+    landed(T2.at[:, 0:64 * (GZ - 1)], S2.at[0:GZ - 1], a2s, a2r)
 
     @pl.loop(0, LZ // 2)
     def _(p):
@@ -274,19 +311,30 @@
             phi = right(c, bhi[...], blo[...])
             z = 2 * p + q
             Pf[z + 1] = phi[:, :N]
-            PS[pl.ds((z // 4) * 16, 16), lax.rem(z, 4)] = phi[:, N:].reshape(16, 8, N)
+            PS[pl.ds((z // 4) * 16, 16), (2 - lax.rem(p, 2)) if q else 3 * lax.rem(p, 2)] = phi[:, N:].reshape(16, 8, N)
 
     def phis(i):
         p = vpeer(i)
         return pltpu.make_async_remote_copy(
-            PS.at[p], RE.at[v, 1:5], fs.at[i], fr.at[i], device_id=(p, g), device_id_type=MESH)
+            PS.at[p, 0:2], RE.at[v, 1:3], fs, fr, device_id=(p, g), device_id_type=MESH)
+
+    def phis2(i):
+        p = vpeer(i)
+        return pltpu.make_async_remote_copy(
+            PS.at[p, 2:4], RE.at[v, 4:6], f2s, f2r, device_id=(p, g), device_id_type=MESH)
 
     @pl.loop(1, NV)
     def _(i):
         phis(i).start()
 
-    mine = pltpu.make_async_copy(PS.at[v], RE.at[v, 1:5], lsem.at[0])
+    @pl.loop(1, NV)
+    def _(i):
+        phis2(i).start()
+
+    mine = pltpu.make_async_copy(PS.at[v, 0:2], RE.at[v, 1:3], lsem.at[0])
     mine.start()
+    mine2 = pltpu.make_async_copy(PS.at[v, 2:4], RE.at[v, 4:6], lsem.at[6])
+    mine2.start()
 
     y8 = pl.multiple_of((v // 2) * 8, 8)
     odd = lax.rem(v, 2) == 1
@@ -306,60 +354,50 @@
     edge0.wait()
     edge1.wait()
 
-    @pl.loop(0, LZ)
-    def _(z):
+    @pl.loop(0, LZ // 2)
+    def _(p):
         rows = pl.ds(y8, 8)
-        grads = (BN[0, z, rows], BN[1, z, rows], Pf[z + 2, rows] - Pf[z, rows])
         for c in range(3):
-            blk = E[c, z + 2, rows] + time_step * (Rt[c, z + 1, rows] - grads[c] * half_inv)
-            base_out[c, z] = jnp.where(odd, blk[4:8], blk[0:4])
+            pair = []
+            for q in range(2):
+                z = 2 * p + q
+                grad = (Pf[z + 2, rows] - Pf[z, rows]) if c == 2 else BN[c, z, rows]
+                blk = E[c, z + 2, rows] + time_step * (Rt[c, z + 1, rows] - grad * half_inv)
+                pair.append(jnp.where(odd, blk[4:8], blk[0:4]))
+            base_out[pl.ds(pl.multiple_of(c * 4 * LZ + p * 8, 8), 8), :] = jnp.concatenate(pair, axis=0)
 
     mine.wait()
-
-    @pl.loop(1, NV)
-    def _(i):
-        phis(i).wait()
-
-    for z in range(4):
-        hsend[0, z * NV:(z + 1) * NV] = RE[:, z + 1, 7, :]
-        hsend[1, z * NV:(z + 1) * NV] = RE[:, z + 1, 0, :]
+    keep.wait()
+
+    landed(YS.at[0:NV - 1, :, 0], R.at[0:NV - 1, :, 0], xs, xr)
+
+    landed(YS.at[0:NV - 1, :, 0:2], R.at[0:NV - 1, :, 0:2], ys, yr)
+
+    landed(YS.at[0:NV - 1, :, 0], R.at[0:NV - 1, :, 0], es, er)
+
+    landed(PS.at[0:NV - 1, 0:2], RE.at[0:NV - 1, 1:3], fs, fr)
+
     rimhi = half * 16 + lax.rem(ring + 1, 16)
     rimlo = half * 16 + lax.rem(ring + 15, 16)
     rims = [
         pltpu.make_async_remote_copy(hsend.at[0], hrecv.at[0], ns.at[0], nr.at[0], device_id=(rimhi, g), device_id_type=MESH),
         pltpu.make_async_remote_copy(hsend.at[1], hrecv.at[1], ns.at[1], nr.at[1], device_id=(rimlo, g), device_id_type=MESH),
-        pltpu.make_async_remote_copy(RE.at[:, 4], RE.at[:, 0], ns.at[2], nr.at[2], device_id=above, device_id_type=MESH),
-        pltpu.make_async_remote_copy(RE.at[:, 1], RE.at[:, 5], ns.at[3], nr.at[3], device_id=below, device_id_type=MESH),
+        pltpu.make_async_remote_copy(RE.at[:, 2], RE.at[:, 0], ns.at[2], nr.at[2], device_id=above, device_id_type=MESH),
+        pltpu.make_async_remote_copy(RE.at[:, 1], RE.at[:, 3], ns.at[3], nr.at[3], device_id=below, device_id_type=MESH),
     ]
-    for c in rims:
-        c.start()
-    keep.wait()
-
-    @pl.loop(1, NV)
-    def _(i):
-        inner(i).wait()
-
-    @pl.loop(1, NV)
-    def _(i):
-        outer(i).wait()
-
-    for c in rims:
-        c.wait()
-    HB[pl.ds(0, N, stride=8), :] = hrecv[0]
-    HB[pl.ds(7, N, stride=8), :] = hrecv[1]
+    rims[2].start()
+    rims[3].start()
+    mine2.wait()
+
+    landed(PS.at[0:NV - 1, 2:4], RE.at[0:NV - 1, 4:6], f2s, f2r)
+
+    slot = (0, 1, 4, 5, 2, 3)
+    for z in range(4):
+        hsend[0, z * NV:(z + 1) * NV] = RE[:, slot[z + 1], 7, :]
+        hsend[1, z * NV:(z + 1) * NV] = RE[:, slot[z + 1], 0, :]
+    rims[0].start()
+    rims[1].start()
     sub = lax.broadcasted_iota(jnp.int32, (8, N), 0)
-
-    @pl.loop(0, NV)
-    def _(j):
-        for z in range(4):
-            phi = RE[j, z + 1]
-            rim = HB[pl.ds(pl.multiple_of((z * NV + j) * 8, 8), 8), :]
-            yp = jnp.where(sub == 7, rim, pltpu.roll(phi, 7, 0))
-            ym = jnp.where(sub == 0, rim, pltpu.roll(phi, 1, 0))
-            grads = (up(phi, 1) - down(phi, 1), yp - ym, RE[j, z + 2] - RE[j, z])
-            for c in range(3):
-                V2[pl.ds(pl.multiple_of(j * ROWS + c * 32 + z * 8, 8), 8), :] = (
-                    R[j, c, z] - (time_step * half_inv) * grads[c])
 
     def gram_step(k, acc):
         cols = [V2[pl.ds(8 * k + j, NV, stride=ROWS), :] for j in range(8)]
@@ -368,7 +406,31 @@
         return acc + lax.dot_general(x, x, (((1,), (1,)), ((), ())), precision=lax.Precision.HIGHEST,
                                      preferred_element_type=f32)
 
-    gram = lax.fori_loop(0, ROWS // 8, gram_step, jnp.zeros((NV, NV), f32))
+    def form(c, acc):
+        @pl.loop(0, NV)
+        def _(j):
+            for z in range(4):
+                phi = RE[j, slot[z + 1]]
+                if c == 0:
+                    grad = up(phi, 1) - down(phi, 1)
+                elif c == 1:
+                    rim = HB[pl.ds(pl.multiple_of((z * NV + j) * 8, 8), 8), :]
+                    grad = jnp.where(sub == 7, rim, pltpu.roll(phi, 7, 0)) - jnp.where(sub == 0, rim, pltpu.roll(phi, 1, 0))
+                else:
+                    grad = RE[j, slot[z + 2]] - RE[j, slot[z]]
+                V2[pl.ds(pl.multiple_of(j * ROWS + c * 32 + z * 8, 8), 8), :] = R[j, c, z] - (time_step * half_inv) * grad
+
+        return lax.fori_loop(4 * c, 4 * c + 4, gram_step, acc)
+
+    gram = form(0, jnp.zeros((NV, NV), f32))
+    rims[2].wait()
+    rims[3].wait()
+    gram = form(2, gram)
+    rims[0].wait()
+    rims[1].wait()
+    HB[pl.ds(0, N, stride=8), :] = hrecv[0]
+    HB[pl.ds(7, N, stride=8), :] = hrecv[1]
+    gram = form(1, gram)
     gbuf[...] = jnp.zeros((NV, N), f32)
     gbuf[:, 0:NV] = gram
     full = gbuf[...]
@@ -381,15 +443,13 @@
 
     def ex1(i):
         return pltpu.make_async_remote_copy(
-            gsend, grecv.at[g], gs.at[i], gr.at[i], device_id=(v, zpeer(i)), device_id_type=MESH)
+            gsend, grecv.at[g], gs, gr, device_id=(v, zpeer(i)), device_id_type=MESH)
 
     @pl.loop(1, GZ)
     def _(i):
         ex1(i).start()
 
-    @pl.loop(1, GZ)
-    def _(i):
-        ex1(i).wait()
+    landed(grecv.at[0:GZ - 1], grecv.at[0:GZ - 1], gs, gr)
 
     total = grecv[0]
     for i in range(1, GZ):
@@ -399,15 +459,13 @@
 
     def ex2(i):
         return pltpu.make_async_remote_copy(
-            vsend, vrecv.at[v], ws.at[i], wr.at[i], device_id=(vpeer(i), g), device_id_type=MESH)
-
-    @pl.loop(1, NV)
-    def _(i):
-        ex2(i).start()
-
-    @pl.loop(1, NV)
-    def _(i):
-        ex2(i).wait()
+            vsend, vrecv.at[v], ws, wr, device_id=(vpeer(i), g), device_id_type=MESH)
+
+    @pl.loop(0, NV - 1)
+    def _(t):
+        ex2(far(t)).start()
+
+    landed(vrecv.at[0:NV - 1], vrecv.at[0:NV - 1], ws, wr)
 
     total = vrecv[0]
     for i in range(1, NV):
@@ -426,59 +484,54 @@
     diag = jnp.where(lane == row, m, 0.0)
     dcol = jnp.sum(diag, axis=1, keepdims=True)
     drow = jnp.sum(diag, axis=0, keepdims=True)
-    growth[...] = 0.5 * jnp.log(drow[:, 0:NV])
+    growth[...] = (0.5 * jnp.log(drow))[0, 0:NV]
     inv = pltpu.roll(m, N - NV, 1) * (1.0 / jnp.sqrt(dcol))
     inv = inv[:, 0:NV]
 
-    @pl.loop(0, ROWS // 8)
-    def _(k):
-        o = lax.dot_general(inv, X[k], (((1,), (0,)), ((), ())), precision=lax.Precision.HIGHEST,
-                            preferred_element_type=f32)
-        for j in range(8):
-            O2[pl.ds(8 * k + j, NV, stride=ROWS), :] = o[:, j * N:(j + 1) * N]
-
-    @pl.loop(0, NV)
-    def _(i):
-        for c in range(3):
-            for z in range(4):
-                O5[i, c, z] = O2[pl.ds(pl.multiple_of(i * ROWS + c * 32 + z * 8, 8), 8), :]
-
-    def a2a4(i):
+    def a2a4(c, i):
         p = vpeer(i)
         return pltpu.make_async_remote_copy(
-            O5.at[p], ortho.at[:, pl.ds(half * 4, 4), ring],
-            os_.at[i], or_.at[i], device_id=(p, g), device_id_type=MESH)
-
-    @pl.loop(1, NV)
-    def _(i):
-        a2a4(i).start()
+            O5.at[p, c], ortho.at[c, pl.ds(half * 4, 4), ring],
+            os_, or_, device_id=(p, g), device_id_type=MESH)
+
+    for c in range(3):
+        @pl.loop(0, 4)
+        def _(z):
+            o = lax.dot_general(inv, X[4 * c + z], (((1,), (0,)), ((), ())), precision=lax.Precision.HIGHEST,
+                                preferred_element_type=f32)
+            for j in range(8):
+                O5[:, c, z, j, :] = o[:, j * N:(j + 1) * N]
+
+        @pl.loop(0, NV - 1)
+        def _(t):
+            a2a4(c, far(t)).start()
 
     own = pltpu.make_async_copy(O5.at[v], ortho.at[:, pl.ds(half * 4, 4), ring], lsem.at[1])
     own.start()
     own.wait()
 
-    @pl.loop(1, NV)
-    def _(i):
-        a2a4(i).wait()
+    landed(O5.at[0:NV - 1], O5.at[0:NV - 1], os_, or_)
 
 
 def per_device(base_flow, tangents, shells):
-    ahi, alo, bhi, blo, sine, slope2 = tables()
+    dft, lines = tables()
     vm = pl.BlockSpec(memory_space=pltpu.VMEM)
-    sm = pl.BlockSpec(memory_space=pltpu.SMEM)
     anyspace = pl.BlockSpec(memory_space=pl.ANY)
     dma = pltpu.SemaphoreType.DMA
     plane = (N, N)
     base_rows, ortho, growth = pl.pallas_call(
         kernel,
         out_shape=(
-            jax.ShapeDtypeStruct((3, LZ, N // NV, N), f32),
+            jax.ShapeDtypeStruct((3 * LZ * N // NV, N), f32),
             jax.ShapeDtypeStruct((3, LZ, 16, 8, N), f32),
-            jax.ShapeDtypeStruct((1, NV), f32),
+            jax.ShapeDtypeStruct((NV,), f32),
         ),
-        in_specs=[sm, sm, anyspace, anyspace, vm, vm, vm, vm, vm, vm],
+        in_specs=[anyspace] * 5,
         out_specs=(vm, anyspace, vm),
         scratch_shapes=[
+            pltpu.SMEM((4,), jnp.int32),
+            pltpu.VMEM((4, 2 * N, 2 * N), bf16),
+            pltpu.VMEM((N + 16, N), f32),
             pltpu.VMEM((6, 12) + plane, f32),
             pltpu.VMEM((6, 10) + plane, f32),
             pltpu.VMEM((GZ, 2, 64, N), f32),
@@ -496,36 +549,27 @@
             pltpu.VMEM((8 * N, N), f32),
             pltpu.VMEM((3 * LZ * N, N), f32),
             pltpu.VMEM((ROWS // 8, NV, 8 * N), f32),
-            pltpu.VMEM((3 * LZ * N, N), f32),
             pltpu.VMEM((NV, 3, 4, 8, N), f32),
             pltpu.VMEM((NV, N), f32),
             pltpu.VMEM((8, N), f32),
             pltpu.VMEM((GZ, 8, N), f32),
             pltpu.VMEM((8, N), f32),
             pltpu.VMEM((NV, 8, N), f32),
-            dma((3,)),
+            dma((7,)),
             dma((8,)), dma((8,)),
-            dma((GZ,)), dma((GZ,)),
-            dma((GZ,)), dma((GZ,)),
+            dma(()), dma(()),
+            dma(()), dma(()),
             dma((2,)), dma((2,)),
-            dma((NV,)), dma((NV,)),
-            dma((NV,)), dma((NV,)),
-            dma((NV,)), dma((NV,)),
+        ] + [dma(())] * 10 + [
             dma((4,)), dma((4,)),
-            dma((GZ,)), dma((GZ,)),
-            dma((NV,)), dma((NV,)),
-            dma((NV,)), dma((NV,)),
-        ],
+        ] + [dma(())] * 6,
         compiler_params=pltpu.CompilerParams(
             collective_id=0, has_side_effects=True, vmem_limit_bytes=58 * 1024 * 1024
         ),
     )(
-        shells, jnp.asarray(sine), base_flow, tangents[0],
-        jnp.asarray(ahi), jnp.asarray(alo), jnp.asarray(bhi), jnp.asarray(blo),
-        jnp.asarray(slope2[None, :]),
-        jnp.asarray(np.repeat(slope2[:, None], N, axis=1)),
+        shells, base_flow, tangents[0], jnp.asarray(dft), jnp.asarray(lines),
     )
-    return base_rows, ortho.reshape(tangents.shape), growth[0]
+    return base_rows.reshape(3, LZ, N // NV, N), ortho.reshape(tangents.shape), growth
 
 
 def solution(mesh):

time: 228 us -> 214 us (0.939)
  Pallas kernels: 222 us -> 208 us
    pallas_call x1, Pallas kernels: 222 us -> 208 us  [per_device(): pl.pallas_call(kernel, out_shape=(jax.ShapeDtypeStruct((3 * LZ * N // NV,...]
where the time goes in v3:
time: 214 us; the launch traced here: 213 us
  Pallas kernels  208 us (97%)
  local copies, waits for them, and re-layouts  4.64 us (2%)
    pallas_call x1, Pallas kernels, per_device(): pl.pallas_call(kernel, out_shape=(jax.ShapeDtypeStruct((3 * LZ * N // NV,...  208 us
    unnamed x5, local copies, waits for them, and re-layouts  4.64 us

profile of v3, /device:TPU:1, one launch (start us, length us, event | category | flops | bytes accessed | tf_op | source)
XLA Modules:
  0.0 213.5 jit_solution(4456507856319714162)
XLA Ops:
  0.6 208.2 %shard_map.76 = (f32[96,128]{1,0:T(8,128)}, f32[3,8,16,8,128]{4,3,2,1,0:T(8,128)}, f32[32]{0:T(128)}) custom-call(s32[4]{0:T(128)} %shells_in.1, f32[3,8,128,128]{3,2,1,0:T(8,128)} %base.1, f32[3,8,128,128]{3,2,1,0:T(8,128)} %bitcast.4, bf16[4,256,256]{2,1,0:T(8,128)(2,1)} %constant.4.clone.dft_in, f32[144,128]{1,0:T(8,128)} %constant.5.clone.lines_in), custom_call_target="tpu_custom_call" | custom-call | tf_op jit(solution)/shard_map/pallas_call | solution.py:522
  208.8 1.4 copy.11
  210.3 0.0 copy-start
  210.3 2.7 %copy.12 = f32[1,3,8,128,128]{4,3,2,1,0:T(8,128)} copy(f32[1,3,8,128,128]{4,3,2,1,0:T(8,128)} %bitcast.3) | data formatting | bytes 3145728
  213.0 0.0 copy-done
  213.0 0.5 copy.13
Async XLA Ops:
  210.3 2.7 %copy-start = (f32[32]{0:T(128)S(1)}, f32[32]{0:T(128)}, u32[]{:S(2)}) copy-start(f32[32]{0:T(128)} %get-tuple-element.14) | copy-start | bytes 388

commit v4 on v3

--- a/solution.py
+++ b/solution.py
@@ -522,12 +522,12 @@
     base_rows, ortho, growth = pl.pallas_call(
         kernel,
         out_shape=(
-            jax.ShapeDtypeStruct((3 * LZ * N // NV, N), f32),
-            jax.ShapeDtypeStruct((3, LZ, 16, 8, N), f32),
-            jax.ShapeDtypeStruct((NV,), f32),
+            pltpu.VMEM((3 * LZ * N // NV, N), f32),
+            pltpu.VMEM((3, LZ, 16, 8, N), f32),
+            pltpu.VMEM((NV,), f32),
         ),
         in_specs=[anyspace] * 5,
-        out_specs=(vm, anyspace, vm),
+        out_specs=(vm, vm, vm),
         scratch_shapes=[
             pltpu.SMEM((4,), jnp.int32),
             pltpu.VMEM((4, 2 * N, 2 * N), bf16),

time: 214 us -> 210 us (0.981)
  local copies, waits for them, and re-layouts: 4.64 us -> 2.28 us
    unnamed x5 -> x3, local copies, waits for them, and re-layouts: 4.64 us -> 2.28 us
where the time goes in v4:
time: 210 us
  Pallas kernels  207 us (99%)
  local copies, waits for them, and re-layouts  2.28 us (1%)
    pallas_call x1, Pallas kernels, per_device(): pl.pallas_call(kernel, out_shape=(pltpu.VMEM((3 * LZ * N // NV, N), f32),...  207 us

profile of v4, /device:TPU:1, one launch (start us, length us, event | category | flops | bytes accessed | tf_op | source)
XLA Modules:
  0.0 210.3 jit_solution(2101255921985814961)
XLA Ops:
  0.6 207.4 %shard_map.76 = (f32[96,128]{1,0:T(8,128)S(1)}, f32[3,8,16,8,128]{4,3,2,1,0:T(8,128)S(1)}, f32[32]{0:T(128)S(1)}) custom-call(s32[4]{0:T(128)} %shells_in.1, f32[3,8,128,128]{3,2,1,0:T(8,128)} %base.1, f32[3,8,128,128]{3,2,1,0:T(8,128)} %bitcast.5, bf16[4,256,256]{2,1,0:T(8,128)(2,1)} %constant.4.clone.dft_in, f32[144,128]{1,0:T(8,128)} %constant.5.clone.lines_in), custom_call_target="tpu_custom_call" | custom-call | tf_op jit(solution)/shard_map/pallas_call | solution.py:522
  208.0 0.6 copy.11
  208.6 1.1 copy.12
  209.8 0.5 copy.13
